TPU v7x, 256 devices: a whole 4x4x8 slice. The times are simulated.
256 devices in a mesh: pairs: 16 (over z, core), cols: 16 (over y, x).
Axes of the slice: x: 4, y: 4, z: 8, core: 2. Of those that a mesh axis runs over, the one named last changes fastest.
Arguments:
- pair_list: int32 [96, 5], P('pairs'), may hold values from 0 to 15, as said below
- near_tile_block: bfloat16 [96, 2048, 2048], P('pairs', None, 'cols'), may hold values from -0.0546875 to 0.0546875
- history: float32 [4, 32, 32, 2048], P(None, 'pairs', None, 'cols'), may hold values from -6 to 6
- excitation: float32 [4, 32, 32, 2048], P(None, 'pairs', None, 'cols'), may hold values from -6 to 6
- diagonal: float32 [32, 2048], P('pairs', 'cols'), may hold values from 2 to 4
Outputs:
- densities: float32 [4, 32, 32, 2048], P(None, 'pairs', None, 'cols')
Inputs may be any that keep to these rules, and one draw needn't show every extreme that they name: `pair_list`: rows s * 6 to s * 6 + 5 are the slots of index s of pairs. Column 0 and column 2 are below 2, column 1 below 16, column 3 below 4, column 4 is 0 or 1. The live slots of a device come first and number at least 3; among them no value of column 1 appears more than 3 times, and some value exactly 3 times. One device has all 6 slots live.
All inputs are finite; a program needn't handle non-finite values.
Results may differ from a plain program's by a relative error of at most 0.0018.
Values may be sent and summed in bfloat16 or wider, within the bound.
A program may use at most 64 MiB of HBM per device.

v0:
```python
import jax
import jax.numpy as jnp
from jax import lax
from jax.sharding import PartitionSpec as P

SM = 3
STEPS = 4


def shards(pair_list, near_tile_block, history, excitation, diagonal):
    groups = lax.axis_size("pairs")
    delays, clusters, excite, width = history.shape
    buffer_rows = groups * SM
    first_local = pair_list[:, 0]
    owners = pair_list[:, 1]
    second_local = pair_list[:, 2]
    delay_index = pair_list[:, 3]
    live = pair_list[:, 4] == 1
    live_float = live.astype(jnp.float32)
    owner_hits = ((owners[:, None] == jnp.arange(groups)[None, :]) & live[:, None]).astype(
        jnp.int32
    )
    rank = jnp.sum(jnp.cumsum(owner_hits, axis=0) * owner_hits, axis=1) - 1
    position = jnp.where(live, owners * SM + rank, buffer_rows)
    codes = jnp.full((buffer_rows,), -1, jnp.int32)
    codes = codes.at[position].set(delay_index * clusters + second_local, mode="drop")
    wanted = lax.all_to_all(
        codes.reshape(groups, SM), "pairs", split_axis=0, concat_axis=0, tiled=True
    ).reshape(buffer_rows)
    wanted_valid = wanted >= 0
    wanted_index = jnp.maximum(wanted, 0)
    back_table = (
        (wanted_index[None, :] % clusters == jnp.arange(clusters)[:, None]) & wanted_valid[None, :]
    ).astype(jnp.float32)
    first_table = (first_local[None, :] == jnp.arange(clusters)[:, None]).astype(
        jnp.float32
    ) * live_float[None, :]
    slot_source = jnp.minimum(position, buffer_rows - 1)
    own_index = delay_index * clusters + first_local
    results = []
    for step in range(STEPS):
        rounded = history.astype(jnp.bfloat16)
        flat = rounded.reshape(delays * clusters, excite, width)
        outgoing = jnp.where(
            wanted_valid[:, None, None],
            jnp.take(flat, wanted_index, axis=0),
            jnp.zeros((), jnp.bfloat16),
        )
        incoming = lax.all_to_all(
            outgoing.reshape(groups, SM, excite, width),
            "pairs",
            split_axis=0,
            concat_axis=0,
            tiled=True,
        )
        remote = jnp.take(incoming.reshape(buffer_rows, excite, width), slot_source, axis=0)
        forward = jnp.einsum(
            "sek,smk->sem", remote, near_tile_block, preferred_element_type=jnp.float32
        )
        forward_sum = jnp.einsum(
            "cs,sem->cem", first_table, forward, precision=lax.Precision.HIGHEST
        )
        collected = lax.all_gather(rounded, "cols", axis=3, tiled=True)
        near_rows = jnp.take(collected.reshape(delays * clusters, excite, -1), own_index, axis=0)
        backward = jnp.einsum(
            "sem,smk->sek", near_rows, near_tile_block, preferred_element_type=jnp.float32
        )
        backward = backward * live_float[:, None, None]
        outbound = (
            jnp.zeros((buffer_rows, excite, width), jnp.float32)
            .at[position]
            .set(backward, mode="drop")
        )
        received = lax.all_to_all(
            outbound.reshape(groups, SM, excite, width),
            "pairs",
            split_axis=0,
            concat_axis=0,
            tiled=True,
        )
        backward_sum = jnp.einsum(
            "cq,qek->cek",
            back_table,
            received.reshape(buffer_rows, excite, width),
            precision=lax.Precision.HIGHEST,
        )
        total = lax.psum(forward_sum, "cols")
        own_part = lax.dynamic_slice_in_dim(total, lax.axis_index("cols") * width, width, 2)
        field = own_part + backward_sum
        fresh = (excitation[step] - field) / diagonal[:, None, :]
        results.append(fresh)
        history = jnp.concatenate([fresh[None], history[:-1]], axis=0)
    return jnp.stack(results)


def solution(mesh):
    placed = (
        P("pairs", None),
        P("pairs", None, "cols"),
        P(None, "pairs", None, "cols"),
        P(None, "pairs", None, "cols"),
        P("pairs", "cols"),
    )
    return jax.shard_map(
        shards,
        mesh=mesh,
        in_specs=placed,
        out_specs=P(None, "pairs", None, "cols"),
        check_vma=False,
    )
```

profile of v0, /device:TPU:1, one launch (start us, length us, event | category | flops | bytes accessed | tf_op | source)
XLA Modules:
  0.0 695.9 jit_solution(621412180078924286)
XLA Ops:
  11.3 16.8 %all_to_all.49 = s32[16,1,3]{2,1,0:T(1,128)S(1)} all-to-all(s32[16,1,3]{2,1,0:T(1,128)S(1)} %bitcast.106), channel_id=1, replica_groups=mesh['pairs'=16,'cols'=16] {'pairs'}, dimensions={0} | all-to-all | bytes 384 | tf_op jit(solution)/shard_map/all_to_all | solution.py:27
  32.7 4.0 all-to-all-start.1
  38.5 21.6 %all-gather.5.cloned.1.call-done = bf16[4,2,32,2048]{3,2,1,0:T(8,128)(2,1)} async-done(((bf16[4,2,32,128]{3,2,1,0:T(8,128)(2,1)}), bf16[4,2,32,2048]{3,2,1,0:T(8,128)(2,1)}) %all-gather.5.cloned.1.call-update) | async-done | bytes 1048592 | tf_op jit(solution)/shard_map/all_gather | solution.py:63
  60.1 2.8 gather_fusion.2
  62.9 2.4 convolution_multiply_fusion.3
  66.3 2.2 scatter_fusion
  68.5 9.3 %all-to-all-start.2 = ((f32[16,3,32,128]{3,2,1,0:T(8,128)}), f32[16,3,32,128]{3,2,1,0:T(8,128)}, u32[]{:S(2)}, u32[]{:S(2)}) async-start(f32[16,3,32,128]{3,2,1,0:T(8,128)} %bitcast.95), calls=%async_computation.2 | async-start | bytes 1572864 | tf_op jit(solution)/shard_map/all_to_all | solution.py:74
  82.6 3.5 fusion.6
  87.7 91.2 %all-reduce.5.cloned.1.call-done = f32[2,32,2048]{2,0,1:T(2,128)} async-done(((f32[2,32,2048]{2,0,1:T(2,128)}), f32[2,32,2048]{2,0,1:T(2,128)}) %all-reduce.5.cloned.1.call-update) | async-done | bytes 524304 | tf_op jit(solution)/shard_map/psum | solution.py:87
  185.3 9.7 %all-to-all-start.3 = ((bf16[16,3,32,128]{3,2,1,0:T(8,128)(2,1)}), bf16[16,3,32,128]{3,2,1,0:T(8,128)(2,1)S(1)}, u32[]{:S(2)}, u32[]{:S(2)}) async-start(bf16[16,3,32,128]{3,2,1,0:T(8,128)(2,1)} %bitcast.17), calls=%async_computation.3 | async-start | bytes 786432 | tf_op jit(solution)/shard_map/all_to_all | solution.py:49
  195.0 35.3 %all-gather.7.cloned.1.call-done = bf16[4,2,32,2048]{3,2,1,0:T(8,128)(2,1)} async-done(((bf16[4,2,32,128]{3,2,1,0:T(8,128)(2,1)}), bf16[4,2,32,2048]{3,2,1,0:T(8,128)(2,1)}) %all-gather.7.cloned.1.call-update) | async-done | bytes 1048592 | tf_op jit(solution)/shard_map/all_gather | solution.py:63
  230.3 2.8 gather_fusion.5
  233.1 2.4 convolution_multiply_fusion.2
  236.5 2.3 scatter_fusion.1
  238.8 9.3 %all-to-all-start.4 = ((f32[16,3,32,128]{3,2,1,0:T(8,128)}), f32[16,3,32,128]{3,2,1,0:T(8,128)}, u32[]{:S(2)}, u32[]{:S(2)}) async-start(f32[16,3,32,128]{3,2,1,0:T(8,128)} %bitcast.96), calls=%async_computation.4 | async-start | bytes 1572864 | tf_op jit(solution)/shard_map/all_to_all | solution.py:74
  251.8 3.5 fusion.4
  255.4 92.8 %all-reduce.7.cloned.1.call-done = f32[2,32,2048]{2,0,1:T(2,128)} async-done(((f32[2,32,2048]{2,0,1:T(2,128)}), f32[2,32,2048]{2,0,1:T(2,128)}) %all-reduce.7.cloned.1.call-update) | async-done | bytes 524304 | tf_op jit(solution)/shard_map/psum | solution.py:87
  354.5 9.7 %all-to-all-start.5 = ((bf16[16,3,32,128]{3,2,1,0:T(8,128)(2,1)}), bf16[16,3,32,128]{3,2,1,0:T(8,128)(2,1)S(1)}, u32[]{:S(2)}, u32[]{:S(2)}) async-start(bf16[16,3,32,128]{3,2,1,0:T(8,128)(2,1)} %bitcast.25), calls=%async_computation.5 | async-start | bytes 786432 | tf_op jit(solution)/shard_map/all_to_all | solution.py:49
  364.2 35.3 %all-gather.9.cloned.1.call-done = bf16[4,2,32,2048]{3,2,1,0:T(8,128)(2,1)} async-done(((bf16[4,2,32,128]{3,2,1,0:T(8,128)(2,1)}), bf16[4,2,32,2048]{3,2,1,0:T(8,128)(2,1)}) %all-gather.9.cloned.1.call-update) | async-done | bytes 1048592 | tf_op jit(solution)/shard_map/all_gather | solution.py:63
  399.5 2.8 gather_fusion.8
  402.3 2.4 convolution_multiply_fusion.1
  405.8 2.3 scatter_fusion.2
  408.1 9.3 %all-to-all-start.6 = ((f32[16,3,32,128]{3,2,1,0:T(8,128)}), f32[16,3,32,128]{3,2,1,0:T(8,128)}, u32[]{:S(2)}, u32[]{:S(2)}) async-start(f32[16,3,32,128]{3,2,1,0:T(8,128)} %bitcast.97), calls=%async_computation.6 | async-start | bytes 1572864 | tf_op jit(solution)/shard_map/all_to_all | solution.py:74
  420.8 3.5 fusion.2
  424.4 92.8 %all-reduce.9.cloned.1.call-done = f32[2,32,2048]{2,0,1:T(2,128)} async-done(((f32[2,32,2048]{2,0,1:T(2,128)}), f32[2,32,2048]{2,0,1:T(2,128)}) %all-reduce.9.cloned.1.call-update) | async-done | bytes 524304 | tf_op jit(solution)/shard_map/psum | solution.py:87
  523.6 9.7 %all-to-all-start.7 = ((bf16[16,3,32,128]{3,2,1,0:T(8,128)(2,1)}), bf16[16,3,32,128]{3,2,1,0:T(8,128)(2,1)S(1)}, u32[]{:S(2)}, u32[]{:S(2)}) async-start(bf16[16,3,32,128]{3,2,1,0:T(8,128)(2,1)} %bitcast.33), calls=%async_computation.7 | async-start | bytes 786432 | tf_op jit(solution)/shard_map/all_to_all | solution.py:49
  533.3 35.3 %all-gather.11.cloned.1.call-done = bf16[4,2,32,2048]{3,2,1,0:T(8,128)(2,1)} async-done(((bf16[4,2,32,128]{3,2,1,0:T(8,128)(2,1)}), bf16[4,2,32,2048]{3,2,1,0:T(8,128)(2,1)}) %all-gather.11.cloned.1.call-update) | async-done | bytes 1048592 | tf_op jit(solution)/shard_map/all_gather | solution.py:63
  568.6 2.8 gather_fusion.11
  571.4 2.4 convolution_multiply_fusion
  577.0 9.3 %all-to-all-start.8 = ((f32[16,3,32,128]{3,2,1,0:T(8,128)}), f32[16,3,32,128]{3,2,1,0:T(8,128)}, u32[]{:S(2)}, u32[]{:S(2)}) async-start(f32[16,3,32,128]{3,2,1,0:T(8,128)} %bitcast.94), calls=%async_computation.8 | async-start | bytes 1572864 | tf_op jit(solution)/shard_map/all_to_all | solution.py:74
  590.0 3.5 fusion
  593.5 92.8 %all-reduce.11.cloned.1.call-done = f32[2,32,2048]{2,0,1:T(2,128)} async-done(((f32[2,32,2048]{2,0,1:T(2,128)}), f32[2,32,2048]{2,0,1:T(2,128)}) %all-reduce.11.cloned.1.call-update) | async-done | bytes 524304 | tf_op jit(solution)/shard_map/psum | solution.py:87
  (171 shorter events, 55.9 us)
Async XLA Ops:
  6.5 53.5 %all-gather.5.cloned.1.call-start = ((), (), s32[]{:S(2)}) async-start(), calls=%async_computation.10 | async-start | bytes 1114112 | tf_op jit(solution)/shard_map/all_gather | solution.py:63
  32.7 35.9 %all-to-all-start.1 = ((bf16[16,3,32,128]{3,2,1,0:T(8,128)(2,1)}), bf16[16,3,32,128]{3,2,1,0:T(8,128)(2,1)S(1)}, u32[]{:S(2)}, u32[]{:S(2)}) async-start(bf16[16,3,32,128]{3,2,1,0:T(8,128)(2,1)} %bitcast.8), calls=%async_computation.1 | async-start | bytes 786432 | tf_op jit(solution)/shard_map/all_to_all | solution.py:49
  68.5 110.4 %all-to-all-start.2 = ((f32[16,3,32,128]{3,2,1,0:T(8,128)}), f32[16,3,32,128]{3,2,1,0:T(8,128)}, u32[]{:S(2)}, u32[]{:S(2)}) async-start(f32[16,3,32,128]{3,2,1,0:T(8,128)} %bitcast.95), calls=%async_computation.2 | async-start | bytes 1572864 | tf_op jit(solution)/shard_map/all_to_all | solution.py:74
  77.9 101.1 %all-reduce.5.cloned.1.call-start = ((), (), s32[]{:S(2)}) async-start(), calls=%async_computation.9 | async-start | bytes 1048576 | tf_op jit(solution)/shard_map/psum | solution.py:87
  80.5 98.4 %copy-start.23 = (f32[2,128]{1,0:T(2,128)S(1)}, f32[2,128]{1,0:T(2,128)}, u32[]{:S(2)}) copy-start(f32[2,128]{1,0:T(2,128)} %param.15) | copy-start | bytes 3076
  86.1 144.2 %all-gather.7.cloned.1.call-start = ((), (), s32[]{:S(2)}) async-start(), calls=%async_computation.12 | async-start | bytes 1114112 | tf_op jit(solution)/shard_map/all_gather | solution.py:63
  87.0 95.1 %copy-start.1 = (bf16[3,2,32,128]{3,2,1,0:T(8,128)(2,1)}, bf16[3,2,32,128]{3,2,1,0:T(8,128)(2,1)S(1)}, u32[]{:S(2)}) copy-start(bf16[3,2,32,128]{3,2,1,0:T(8,128)(2,1)S(1)} %slice.43) | copy-start | bytes 147460
  87.7 94.4 %copy-start.33 = (pred[2,48]{1,0:T(4,128)(4,1)}, pred[2,48]{1,0:T(4,128)(4,1)S(1)}, u32[]{:S(2)}) copy-start(pred[2,48]{1,0:T(4,128)(4,1)S(1)} %compare_and_fusion.3) | copy-start | bytes 292
  185.3 53.5 %all-to-all-start.3 = ((bf16[16,3,32,128]{3,2,1,0:T(8,128)(2,1)}), bf16[16,3,32,128]{3,2,1,0:T(8,128)(2,1)S(1)}, u32[]{:S(2)}, u32[]{:S(2)}) async-start(bf16[16,3,32,128]{3,2,1,0:T(8,128)(2,1)} %bitcast.17), calls=%async_computation.3 | async-start | bytes 786432 | tf_op jit(solution)/shard_map/all_to_all | solution.py:49
  238.8 109.3 %all-to-all-start.4 = ((f32[16,3,32,128]{3,2,1,0:T(8,128)}), f32[16,3,32,128]{3,2,1,0:T(8,128)}, u32[]{:S(2)}, u32[]{:S(2)}) async-start(f32[16,3,32,128]{3,2,1,0:T(8,128)} %bitcast.96), calls=%async_computation.4 | async-start | bytes 1572864 | tf_op jit(solution)/shard_map/all_to_all | solution.py:74
  248.2 100.0 %all-reduce.7.cloned.1.call-start = ((), (), s32[]{:S(2)}) async-start(), calls=%async_computation.11 | async-start | bytes 1048576 | tf_op jit(solution)/shard_map/psum | solution.py:87
  249.7 98.4 %copy-start.13 = (f32[1,2,32,128]{3,2,1,0:T(8,128)S(1)}, f32[1,2,32,128]{3,2,1,0:T(8,128)}, u32[]{:S(2)}) copy-start(f32[1,2,32,128]{3,2,1,0:T(8,128)} %get-tuple-element.17) | copy-start | bytes 98308
  249.7 98.4 %copy-start.24 = (f32[2,128]{1,0:T(2,128)S(1)}, f32[2,128]{1,0:T(2,128)}, u32[]{:S(2)}) copy-start(f32[2,128]{1,0:T(2,128)} %param.15) | copy-start | bytes 3076
  249.7 98.4 %copy-start.34 = (pred[2,48]{1,0:T(4,128)(4,1)S(1)}, pred[2,48]{1,0:T(4,128)(4,1)}, u32[]{:S(2)}) copy-start(pred[2,48]{1,0:T(4,128)(4,1)} %copy-done.33) | copy-start | bytes 292
  255.3 144.2 %all-gather.9.cloned.1.call-start = ((), (), s32[]{:S(2)}) async-start(), calls=%async_computation.14 | async-start | bytes 1114112 | tf_op jit(solution)/shard_map/all_gather | solution.py:63
  255.4 96.0 %copy-start.3 = (bf16[3,2,32,128]{3,2,1,0:T(8,128)(2,1)}, bf16[3,2,32,128]{3,2,1,0:T(8,128)(2,1)S(1)}, u32[]{:S(2)}) copy-start(bf16[3,2,32,128]{3,2,1,0:T(8,128)(2,1)S(1)} %fusion.39) | copy-start | bytes 147460
  354.5 53.5 %all-to-all-start.5 = ((bf16[16,3,32,128]{3,2,1,0:T(8,128)(2,1)}), bf16[16,3,32,128]{3,2,1,0:T(8,128)(2,1)S(1)}, u32[]{:S(2)}, u32[]{:S(2)}) async-start(bf16[16,3,32,128]{3,2,1,0:T(8,128)(2,1)} %bitcast.25), calls=%async_computation.5 | async-start | bytes 786432 | tf_op jit(solution)/shard_map/all_to_all | solution.py:49
  408.1 109.1 %all-to-all-start.6 = ((f32[16,3,32,128]{3,2,1,0:T(8,128)}), f32[16,3,32,128]{3,2,1,0:T(8,128)}, u32[]{:S(2)}, u32[]{:S(2)}) async-start(f32[16,3,32,128]{3,2,1,0:T(8,128)} %bitcast.97), calls=%async_computation.6 | async-start | bytes 1572864 | tf_op jit(solution)/shard_map/all_to_all | solution.py:74
  417.4 99.8 %all-reduce.9.cloned.1.call-start = ((), (), s32[]{:S(2)}) async-start(), calls=%async_computation.13 | async-start | bytes 1048576 | tf_op jit(solution)/shard_map/psum | solution.py:87
  418.8 98.4 %copy-start.12 = (f32[1,2,32,128]{3,2,1,0:T(8,128)S(1)}, f32[1,2,32,128]{3,2,1,0:T(8,128)}, u32[]{:S(2)}) copy-start(f32[1,2,32,128]{3,2,1,0:T(8,128)} %get-tuple-element.16) | copy-start | bytes 98308
  418.8 98.4 %copy-start.25 = (f32[2,128]{1,0:T(2,128)S(1)}, f32[2,128]{1,0:T(2,128)}, u32[]{:S(2)}) copy-start(f32[2,128]{1,0:T(2,128)} %param.15) | copy-start | bytes 3076
  418.8 98.4 %copy-start.35 = (pred[2,48]{1,0:T(4,128)(4,1)S(1)}, pred[2,48]{1,0:T(4,128)(4,1)}, u32[]{:S(2)}) copy-start(pred[2,48]{1,0:T(4,128)(4,1)} %copy-done.33) | copy-start | bytes 292
  424.4 144.2 %all-gather.11.cloned.1.call-start = ((), (), s32[]{:S(2)}) async-start(), calls=%async_computation.16 | async-start | bytes 1114112 | tf_op jit(solution)/shard_map/all_gather | solution.py:63
  523.6 53.4 %all-to-all-start.7 = ((bf16[16,3,32,128]{3,2,1,0:T(8,128)(2,1)}), bf16[16,3,32,128]{3,2,1,0:T(8,128)(2,1)S(1)}, u32[]{:S(2)}, u32[]{:S(2)}) async-start(bf16[16,3,32,128]{3,2,1,0:T(8,128)(2,1)} %bitcast.33), calls=%async_computation.7 | async-start | bytes 786432 | tf_op jit(solution)/shard_map/all_to_all | solution.py:49
  577.0 109.3 %all-to-all-start.8 = ((f32[16,3,32,128]{3,2,1,0:T(8,128)}), f32[16,3,32,128]{3,2,1,0:T(8,128)}, u32[]{:S(2)}, u32[]{:S(2)}) async-start(f32[16,3,32,128]{3,2,1,0:T(8,128)} %bitcast.94), calls=%async_computation.8 | async-start | bytes 1572864 | tf_op jit(solution)/shard_map/all_to_all | solution.py:74
  586.4 100.0 %all-reduce.11.cloned.1.call-start = ((), (), s32[]{:S(2)}) async-start(), calls=%async_computation.15 | async-start | bytes 1048576 | tf_op jit(solution)/shard_map/psum | solution.py:87
  587.9 98.4 %copy-start.11 = (f32[1,2,32,128]{3,2,1,0:T(8,128)S(1)}, f32[1,2,32,128]{3,2,1,0:T(8,128)}, u32[]{:S(2)}) copy-start(f32[1,2,32,128]{3,2,1,0:T(8,128)} %get-tuple-element.15) | copy-start | bytes 98308
  587.9 98.4 %copy-start.26 = (f32[2,128]{1,0:T(2,128)S(1)}, f32[2,128]{1,0:T(2,128)}, u32[]{:S(2)}) copy-start(f32[2,128]{1,0:T(2,128)} %param.15) | copy-start | bytes 3076
  587.9 98.4 %copy-start.36 = (pred[2,48]{1,0:T(4,128)(4,1)S(1)}, pred[2,48]{1,0:T(4,128)(4,1)}, u32[]{:S(2)}) copy-start(pred[2,48]{1,0:T(4,128)(4,1)} %copy-done.33) | copy-start | bytes 292
  590.0 98.3 %copy-start.6 = (f32[1,2,32,128]{3,1,2,0:T(2,128)S(1)}, f32[1,2,32,128]{3,1,2,0:T(2,128)}, u32[]{:S(2)}) copy-start(f32[1,2,32,128]{3,1,2,0:T(2,128)} %copy-done.5) | copy-start | bytes 98308
  590.0 98.3 %copy-start.8 = (f32[1,2,32,128]{3,1,2,0:T(2,128)S(1)}, f32[1,2,32,128]{3,1,2,0:T(2,128)}, u32[]{:S(2)}) copy-start(f32[1,2,32,128]{3,1,2,0:T(2,128)} %copy-done.7) | copy-start | bytes 98308
  590.0 98.3 %copy-start.10 = (f32[1,2,32,128]{3,1,2,0:T(2,128)S(1)}, f32[1,2,32,128]{3,1,2,0:T(2,128)}, u32[]{:S(2)}) copy-start(f32[1,2,32,128]{3,1,2,0:T(2,128)} %copy-done.9) | copy-start | bytes 98308
  (27 other events, 431.5 us)
Sparse Core Ops, SparseCore 0:
  9.7 50.2 all-gather.4
  86.2 92.6 all-reduce.4
  182.2 47.9 all-gather.6
  255.4 92.6 all-reduce.6
  351.5 47.9 all-gather.8
  424.5 92.6 all-reduce.8
  520.5 47.9 all-gather.10
  593.6 92.6 all-reduce.10
where the time goes:
time: 699 us; the launch traced here: 696 us
  waiting for transfers between devices  497 us (71%)
  starting transfers between devices  71 us (10%)
  local copies, waits for them, and re-layouts  41.9 us (6%)
  matrix products  39.5 us (6%)
  blocking collectives  16.8 us (2%)
  other arithmetic  15.7 us (2%)
  between operations  14 us (2%)
    psum x4, waiting for transfers between devices, shards(): total = lax.psum(forward_sum, 'cols')  370 us
    all_gather x4, waiting for transfers between devices, shards(): collected = lax.all_gather(rounded, 'cols', axis=3, tiled=True)  127 us
    all_to_all x4, starting transfers between devices, shards(): lax.all_to_all(outbound.reshape(groups, SM, excite, width), 'pairs', spli...  37.3 us
    all_to_all x4, starting transfers between devices, shards(): lax.all_to_all(outgoing.reshape(groups, SM, excite, width), 'pairs', spli...  33 us
    all_to_all x1, blocking collectives, shards(): lax.all_to_all(codes.reshape(groups, SM), 'pairs', split_axis=0, concat_a...  16.8 us
  transfers between devices with their start and end apart: 16, of which 8 were waited for; matrix products, arithmetic and copies ran while one was open for 12% of the time, Pallas kernels for 0%

commit v1 on v0

v1 whole, which is shorter than its diff:
```python
import functools
import math

import jax
import jax.numpy as jnp
from jax import lax
from jax.experimental import pallas as pl
from jax.experimental.pallas import tpu as pltpu
from jax.sharding import PartitionSpec as P

MESH = pl.DeviceIdType.MESH
STEPS = 4
DEL = 4
WIRE = jnp.bfloat16


def ring_distance(offset, size):
    return min(offset, size - offset)


def kernel(
    sizes,
    pair_ref,
    tile_hbm,
    history_hbm,
    excitation_hbm,
    diagonal_hbm,
    out_ref,
    tiles,
    history,
    excitation,
    diagonal,
    by_owner,
    by_col,
    lhs,
    weight,
    product,
    own_back,
    forward_out,
    forward_in,
    sibling_out,
    sibling_in,
    back_out,
    back_in,
    local_sem,
    owner_recv,
    owner_send,
    share_recv,
    share_send,
    col_recv,
    col_send,
    forward_recv,
    forward_send,
    sibling_recv,
    sibling_send,
    back_recv,
    back_send,
):
    depth, rows_y, rows_x, slots, clusters = sizes
    cols = rows_y * rows_x
    width = 128
    pair = lax.axis_index("pairs")
    col = lax.axis_index("cols")
    z, core = pair // 2, lax.rem(pair, 2)
    y, x = col // rows_x, lax.rem(col, rows_x)
    sibling = (z * 2 + 1 - core, col)

    def at_z(dz):
        return lax.rem(z + dz, depth) * 2 + core

    def at_col(dy, dx):
        return lax.rem(y + dy, rows_y) * rows_x + lax.rem(x + dx, rows_x)

    z_far = sorted(range(1, depth), key=lambda d: -ring_distance(d, depth))
    z_near = z_far[::-1]
    col_far = sorted(
        [(dy, dx) for dy in range(rows_y) for dx in range(rows_x)],
        key=lambda d: -ring_distance(d[0], rows_y) - ring_distance(d[1], rows_x),
    )
    peers = [(at_z(dz), col) for dz in z_far] + [sibling]
    peers += [(pair, at_col(dy, dx)) for dy, dx in col_far if (dy, dx) != (0, 0)]

    barrier = pltpu.get_barrier_semaphore()
    for peer in peers:
        pl.semaphore_signal(barrier, inc=1, device_id=peer, device_id_type=MESH)

    loads = [pltpu.make_async_copy(history_hbm, history, local_sem.at[slots])]
    loads += [
        pltpu.make_async_copy(
            tile_hbm.at[s], tiles.at[:, pl.ds(s * width, width)], local_sem.at[s]
        )
        for s in range(slots)
    ]
    loads += [
        pltpu.make_async_copy(excitation_hbm, excitation, local_sem.at[slots + 1]),
        pltpu.make_async_copy(diagonal_hbm, diagonal, local_sem.at[slots + 2]),
    ]
    for load in loads:
        load.start()

    for s in range(slots):
        key = jnp.where(
            pair_ref[s, 4] == 1, pair_ref[s, 1] * clusters + pair_ref[s, 2], -1
        )
        for side in range(2):
            for dz in range(depth):
                owner = lax.rem(z + dz, depth) * 2 + (core if side == 0 else 1 - core)
                for l in range(clusters):
                    weight[((side * depth + dz) * clusters + l) * slots + s] = jnp.where(
                        key == owner * clusters + l, 1.0, 0.0
                    ).astype(jnp.float32)

    loads[0].wait()
    for d in range(DEL):
        rounded = history[d].astype(jnp.bfloat16)
        by_owner[DEL - 1 - d, pair] = rounded
        by_col[DEL - 1 - d, col] = rounded

    pl.semaphore_wait(barrier, len(peers))

    def copy(src, dst, send, recv, device):
        return pltpu.make_async_remote_copy(
            src_ref=src,
            dst_ref=dst,
            send_sem=send,
            recv_sem=recv,
            device_id=device,
            device_id_type=MESH,
        )

    def send_density(phase, first, count):
        times = pl.ds(first, count)
        source = by_owner.at[times, pair]
        for dz in z_far:
            copy(
                source,
                by_owner.at[times, pair],
                owner_send.at[phase],
                owner_recv.at[phase, dz - 1],
                (at_z(dz), col),
            ).start()
        for dy, dx in col_far:
            if (dy, dx) != (0, 0):
                copy(
                    source,
                    by_col.at[times, col],
                    col_send.at[phase],
                    col_recv.at[phase],
                    (pair, at_col(dy, dx)),
                ).start()
        copy(
            source,
            by_owner.at[times, pair],
            share_send.at[phase],
            share_recv.at[phase],
            sibling,
        ).start()

    def wait_recv(ref, sem, send):
        copy(ref, ref, send, sem, sibling).wait_recv()

    def wait_send(ref, sem, recv):
        copy(ref, ref, sem, recv, sibling).wait_send()

    def step(t, first, count):
        times = pl.ds(first, count)
        for dz in z_near:
            source = at_z(depth - dz)
            block = by_owner.at[times, source]
            wait_recv(block, owner_recv.at[t, dz - 1], owner_send.at[t])
            copy(block, block, share_send.at[t], share_recv.at[t], sibling).start()
        wait_recv(by_col.at[times, pl.ds(0, cols - 1)], col_recv.at[t], col_send.at[t])

        for s in range(slots):
            when = t + DEL - 1 - pair_ref[s, 3]
            mine = pair_ref[s, 0]
            near = jnp.concatenate([by_col[when, c, mine] for c in range(cols)], axis=1)
            product[s] = jnp.dot(
                near,
                tiles[:, s * width : (s + 1) * width],
                preferred_element_type=jnp.float32,
            )
        for dz in range(depth):
            for l in range(clusters):
                for side in range(2):
                    base = ((side * depth + dz) * clusters + l) * slots
                    total = weight[base] * product[0]
                    for s in range(1, slots):
                        total += weight[base + s] * product[s]
                    if side == 0:
                        own_back[dz, l] = total
                    else:
                        sibling_out[t, dz, l] = total.astype(WIRE)

        wait_recv(by_owner.at[times, pl.ds(0, depth)], share_recv.at[t], share_send.at[t])
        for s in range(slots):
            when = t + DEL - 1 - pair_ref[s, 3]
            block = by_owner[when, pair_ref[s, 1], pair_ref[s, 2]]
            for l in range(clusters):
                chosen = (pair_ref[s, 4] == 1) & (pair_ref[s, 0] == l)
                lhs[l * 32 : (l + 1) * 32, s * width : (s + 1) * width] = jnp.where(
                    chosen, block, jnp.zeros_like(block)
                )
        copy(
            sibling_out.at[t],
            sibling_in.at[t],
            sibling_send.at[t],
            sibling_recv.at[t],
            sibling,
        ).start()

        field = None
        left = lhs[...]
        for dy, dx in col_far:
            rows = pl.ds(pl.multiple_of(at_col(dy, dx) * width, width), width)
            part = lax.dot_general(
                left,
                tiles[rows, :],
                (((1,), (1,)), ((), ())),
                preferred_element_type=jnp.float32,
            ).reshape(clusters, 32, width)
            if (dy, dx) == (0, 0):
                field = part
            else:
                index = dy * rows_x + dx - 1
                forward_out[t, index] = part.astype(WIRE)
                copy(
                    forward_out.at[t, index],
                    forward_in.at[t, index],
                    forward_send.at[t],
                    forward_recv.at[t],
                    (pair, at_col(dy, dx)),
                ).start()

        wait_recv(sibling_in.at[t], sibling_recv.at[t], sibling_send.at[t])
        for dz in z_far + [0]:
            total = own_back[dz] + sibling_in[t, dz].astype(jnp.float32)
            if dz == 0:
                field = field + total
            else:
                back_out[t, dz - 1] = total.astype(WIRE)
                copy(
                    back_out.at[t, dz - 1],
                    back_in.at[t, dz - 1],
                    back_send.at[t],
                    back_recv.at[t],
                    (at_z(dz), col),
                ).start()

        wait_recv(forward_in.at[t], forward_recv.at[t], forward_send.at[t])
        for index in range(cols - 1):
            field = field + forward_in[t, index].astype(jnp.float32)
        wait_recv(back_in.at[t], back_recv.at[t], back_send.at[t])
        for index in range(depth - 1):
            field = field + back_in[t, index].astype(jnp.float32)
        fresh = (excitation[t] - field) / diagonal[...][:, None, :]
        out_ref[t] = fresh
        return fresh

    def publish(t, fresh):
        rounded = fresh.astype(jnp.bfloat16)
        by_owner[DEL + t, pair] = rounded
        by_col[DEL + t, col] = rounded
        send_density(t + 1, DEL + t, 1)

    send_density(0, 0, DEL)
    for load in loads[1:]:
        load.wait()
    publish(0, step(0, 0, DEL))

    def later(t, carry):
        publish(t, step(t, DEL - 1 + t, 1))
        return carry

    lax.fori_loop(1, STEPS - 1, later, 0)
    step(STEPS - 1, DEL + STEPS - 2, 1)

    for t in range(STEPS):
        times = pl.ds(0, DEL) if t == 0 else pl.ds(DEL - 1 + t, 1)
        wait_send(by_owner.at[times, pl.ds(0, depth - 1)], owner_send.at[t], owner_recv.at[t, 0])
        wait_send(by_owner.at[times, pl.ds(0, depth)], share_send.at[t], share_recv.at[t])
        wait_send(by_col.at[times, pl.ds(0, cols - 1)], col_send.at[t], col_recv.at[t])
        wait_send(forward_out.at[t], forward_send.at[t], forward_recv.at[t])
        wait_send(sibling_out.at[t], sibling_send.at[t], sibling_recv.at[t])
        wait_send(back_out.at[t], back_send.at[t], back_recv.at[t])


def march(groups, cols, pair_list, near_tile_block, history, excitation, diagonal):
    slots, patches, width = near_tile_block.shape
    clusters, excite = history.shape[1:3]
    depth = groups // 2
    rows_y = rows_x = math.isqrt(cols)
    block = (clusters, excite, width)
    dma = pltpu.SemaphoreType.DMA
    anywhere = pl.BlockSpec(memory_space=pl.ANY)
    return pl.pallas_call(
        functools.partial(kernel, (depth, rows_y, rows_x, slots, clusters)),
        out_shape=jax.ShapeDtypeStruct((STEPS,) + block, jnp.float32),
        in_specs=[pl.BlockSpec(memory_space=pltpu.SMEM)] + [anywhere] * 4,
        out_specs=pl.BlockSpec(memory_space=pltpu.VMEM),
        scratch_shapes=[
            pltpu.VMEM((patches, slots * width), jnp.bfloat16),
            pltpu.VMEM((DEL,) + block, jnp.float32),
            pltpu.VMEM((STEPS,) + block, jnp.float32),
            pltpu.VMEM((clusters, width), jnp.float32),
            pltpu.VMEM((DEL + STEPS - 1, groups) + block, jnp.bfloat16),
            pltpu.VMEM((DEL + STEPS - 1, cols) + block, jnp.bfloat16),
            pltpu.VMEM((clusters * excite, slots * width), jnp.bfloat16),
            pltpu.SMEM((groups * clusters * slots,), jnp.float32),
            pltpu.VMEM((slots, excite, width), jnp.float32),
            pltpu.VMEM((depth,) + block, jnp.float32),
            pltpu.VMEM((STEPS, cols - 1) + block, WIRE),
            pltpu.VMEM((STEPS, cols - 1) + block, WIRE),
            pltpu.VMEM((STEPS, depth) + block, WIRE),
            pltpu.VMEM((STEPS, depth) + block, WIRE),
            pltpu.VMEM((STEPS, depth - 1) + block, WIRE),
            pltpu.VMEM((STEPS, depth - 1) + block, WIRE),
            dma((slots + 3,)),
            dma((STEPS, depth - 1)),
            dma((STEPS,)),
            dma((STEPS,)),
            dma((STEPS,)),
            dma((STEPS,)),
            dma((STEPS,)),
            dma((STEPS,)),
            dma((STEPS,)),
            dma((STEPS,)),
            dma((STEPS,)),
            dma((STEPS,)),
            dma((STEPS,)),
        ],
        compiler_params=pltpu.CompilerParams(collective_id=0, has_side_effects=True),
    )(pair_list, near_tile_block, history, excitation, diagonal)


def solution(mesh):
    placed = (
        P("pairs", None),
        P("pairs", None, "cols"),
        P(None, "pairs", None, "cols"),
        P(None, "pairs", None, "cols"),
        P("pairs", "cols"),
    )
    return jax.shard_map(
        functools.partial(march, mesh.shape["pairs"], mesh.shape["cols"]),
        mesh=mesh,
        in_specs=placed,
        out_specs=P(None, "pairs", None, "cols"),
        check_vma=False,
    )
```

time: 699 us -> 84.2 us (0.12)
  waiting for transfers between devices: 497 us -> 0 us
  Pallas kernels: 0 us -> 83.3 us
  starting transfers between devices: 71 us -> 0 us
  local copies, waits for them, and re-layouts: 41.9 us -> 1.57 us
  matrix products: 39.5 us -> 0 us
  blocking collectives: 16.8 us -> 0 us
  other arithmetic: 15.7 us -> 0 us
  between operations: 14 us -> 0.01 us
    psum x4 -> x0, waiting for transfers between devices: 370 us -> none  [shards(): total = lax.psum(forward_sum, 'cols')]
    all_gather x4 -> x0, waiting for transfers between devices: 127 us -> none  [shards(): collected = lax.all_gather(rounded, 'cols', axis=3, tiled=True)]
    pallas_call x0 -> x1, Pallas kernels: none -> 83.3 us  [march(): pl.pallas_call(functools.partial(kernel, (depth, rows_y, rows_x, slots, c...]
    all_to_all x8 -> x0, starting transfers between devices: 70.3 us -> none  [the longest x4 37.3 us: shards(): lax.all_to_all(outbound.reshape(groups, SM, excite, width), 'pairs', spli...]
    dot_general x16 -> x0, matrix products: 39.5 us -> none  [the longest x4 14 us: shards(): jnp.einsum('cs,sem->cem', first_table, forward, precision=lax.Precision.H...]
    gather x12 -> x0, local copies, waits for them, and re-layouts: 22.9 us -> none  [the longest x4 11.4 us: shards(): jnp.take(collected.reshape(delays * clusters, excite, -1), own_index, axi...]
    all_to_all x1 -> x0, blocking collectives: 16.8 us -> none  [shards(): lax.all_to_all(codes.reshape(groups, SM), 'pairs', split_axis=0, concat_a...]
    scatter x5 -> x0, local copies, waits for them, and re-layouts: 9.62 us -> none  [the longest x4 9.03 us: shards(): outbound = jnp.zeros((buffer_rows, excite, width), jnp.float32).at[positi...]
  transfers between devices with their start and end apart: 16 -> 0, of which waited for: 8 -> 0; matrix products, arithmetic and copies ran while one was open for 12% -> 0% of each run, Pallas kernels for 0% -> 0%
where the time goes in v1:
time: 84.2 us; the launch traced here: 84.9 us
  Pallas kernels  83.3 us (99%)
  local copies, waits for them, and re-layouts  1.57 us (2%)
    pallas_call x1, Pallas kernels, march(): pl.pallas_call(functools.partial(kernel, (depth, rows_y, rows_x, slots, c...  83.3 us

profile of v1, /device:TPU:1, one launch (start us, length us, event | category | flops | bytes accessed | tf_op | source)
XLA Modules:
  0.0 84.9 jit_solution(1619410959230274876)
XLA Ops:
  0.0 83.3 %shard_map.55 = f32[4,2,32,128]{3,2,1,0:T(8,128)} custom-call(s32[6,5]{1,0:T(8,128)} %pair_ref.1, bf16[6,2048,128]{2,1,0:T(8,128)(2,1)} %tile_hbm.1, f32[4,2,32,128]{3,2,1,0:T(8,128)} %history_hbm.1, f32[4,2,32,128]{3,2,1,0:T(8,128)} %excitation_hbm.1, f32[2,128]{1,0:T(2,128)} %diagonal_hbm.1), custom_call_target="tpu_custom_call" | custom-call | tf_op jit(solution)/shard_map/pallas_call | solution.py:296
  83.3 1.6 %copy.7 = f32[4,2,32,128]{3,2,1,0:T(8,128)} copy(f32[4,2,32,128]{3,2,1,0:T(8,128)} %shard_map.55) | data formatting | bytes 262144

commit v2 on v1

v2 whole, which is shorter than its diff:
```python
import functools
import math

import jax
import jax.numpy as jnp
from jax import lax
from jax.experimental import pallas as pl
from jax.experimental.pallas import tpu as pltpu
from jax.sharding import PartitionSpec as P

MESH = pl.DeviceIdType.MESH
STEPS = 4
DEL = 4
SM = 3
AHEAD = 2
WIRE = jnp.bfloat16


def ring_distance(offset, size):
    return min(offset, size - offset)


def kernel(
    sizes,
    pair_ref,
    tile_hbm,
    history_hbm,
    excitation_hbm,
    diagonal_hbm,
    out_ref,
    tiles,
    turned,
    history,
    excitation,
    diagonal,
    by_owner,
    near_col,
    far_col,
    drain,
    lhs,
    table,
    product,
    own_back,
    forward_out,
    forward_in,
    sibling_out,
    sibling_in,
    back_out,
    back_in,
    local_sem,
    density_send,
    col_send,
    sum_send,
    early_owner,
    early_share,
    early_col,
    owner_recv,
    share_recv,
    col_recv,
    forward_recv,
    sibling_recv,
    back_recv,
):
    depth, rows_y, rows_x, slots, clusters = sizes
    cols = rows_y * rows_x
    width = 128
    pair = lax.axis_index("pairs")
    col = lax.axis_index("cols")
    z, core = pair // 2, lax.rem(pair, 2)
    y, x = col // rows_x, lax.rem(col, rows_x)
    sibling = (z * 2 + 1 - core, col)

    def at_z(dz):
        return lax.rem(z + dz, depth) * 2 + core

    def at_col(dy, dx):
        return lax.rem(y + dy, rows_y) * rows_x + lax.rem(x + dx, rows_x)

    def z_distance(dz):
        return ring_distance(dz, depth)

    def col_distance(d):
        return ring_distance(d[0], rows_y) + ring_distance(d[1], rows_x)

    z_near = sorted(range(1, depth), key=z_distance)
    z_far = z_near[::-1]
    col_near = sorted(
        [(dy, dx) for dy in range(rows_y) for dx in range(rows_x)][1:], key=col_distance
    )
    col_far = col_near[::-1]
    z_close = sum(z_distance(d) <= 2 for d in z_near)
    col_close = sum(col_distance(d) <= 2 for d in col_near)
    peers = [(at_z(dz), col) for dz in z_far] + [sibling]
    peers += [(pair, at_col(dy, dx)) for dy, dx in col_far]

    barrier = pltpu.get_barrier_semaphore()
    for peer in peers:
        pl.semaphore_signal(barrier, inc=1, device_id=peer, device_id_type=MESH)

    loads = [
        pltpu.make_async_copy(history_hbm, history, local_sem.at[0]),
        pltpu.make_async_copy(excitation_hbm, excitation, local_sem.at[1]),
        pltpu.make_async_copy(diagonal_hbm, diagonal, local_sem.at[2]),
    ]
    for load in loads:
        load.start()
    for s in range(slots):
        pltpu.make_async_copy(
            tile_hbm.at[s], tiles.at[:, pl.ds(s * width, width)], local_sem.at[3]
        ).start()

    loads[0].wait()
    for d in range(DEL):
        rounded = history[d].astype(jnp.bfloat16)
        by_owner[DEL - 1 - d, pair] = rounded
        near_col[DEL - 1 - d, 0] = rounded

    pl.semaphore_wait(barrier, len(peers))

    def copy(src, dst, send, recv, device):
        return pltpu.make_async_remote_copy(
            src_ref=src,
            dst_ref=dst,
            send_sem=send,
            recv_sem=recv,
            device_id=device,
            device_id_type=MESH,
        )

    def arrival(times, index):
        if index < col_close:
            return near_col.at[times, index + 1]
        return far_col.at[times, index - col_close]

    def send_density(times, owner_sem, share_sem, col_sem):
        source = by_owner.at[times, pair]
        for dz in z_far:
            copy(source, source, density_send, owner_sem(dz - 1), (at_z(dz), col)).start()
        for dy, dx in col_far:
            index = col_near.index((dy, dx))
            group = 0 if index < col_close else 1
            target = (pair, at_col(dy, dx))
            copy(source, arrival(times, index), col_send, col_sem(group), target).start()
        copy(source, source, density_send, share_sem, sibling).start()

    def wait_recv(ref, sem):
        copy(ref, ref, density_send, sem, sibling).wait_recv()

    def share(times, dz, owner_sem, share_sem):
        block = by_owner.at[times, at_z(depth - dz)]
        wait_recv(block, owner_sem(dz - 1))
        copy(block, block, density_send, share_sem, sibling).start()

    def send_step(t):
        send_density(
            pl.ds(DEL - 1 + t, 1),
            lambda k: owner_recv.at[t, k],
            share_recv.at[t],
            lambda k: col_recv.at[t, k],
        )

    def early_owner_sem(k):
        return early_owner.at[k]

    def early_col_sem(k):
        return early_col.at[k]

    past = pl.ds(0, DEL - 1)
    send_density(past, early_owner_sem, early_share, early_col_sem)
    send_step(0)

    keys = [
        jnp.where(pair_ref[s, 4] == 1, pair_ref[s, 1] * clusters + pair_ref[s, 2], -1)
        for s in range(slots)
    ]

    def place(n, carry):
        side, rest = n // (depth * clusters), lax.rem(n, depth * clusters)
        dz, l = rest // clusters, lax.rem(rest, clusters)
        owner = lax.rem(z + dz, depth) * 2 + lax.rem(core + side, 2)
        count = jnp.int32(0)
        found = [jnp.int32(slots)] * SM
        for s in range(slots):
            hit = keys[s] == owner * clusters + l
            found = [jnp.where(hit & (count == k), s, found[k]) for k in range(SM)]
            count = jnp.where(hit, count + 1, count)
        for k in range(SM):
            table[n * SM + k] = found[k]
        return carry

    lax.fori_loop(0, 2 * depth * clusters, place, 0)
    product[slots] = jnp.zeros_like(product[slots])
    for load in loads[1:]:
        load.wait()
    pltpu.make_async_copy(tiles, tiles, local_sem.at[3]).wait()

    def turn(c, carry):
        turned[c] = tiles[pl.ds(pl.multiple_of(c * width, width), width), :].T
        return carry

    lax.fori_loop(0, cols, turn, 0)

    for dz in z_near:
        share(past, dz, early_owner_sem, early_share)
    wait_recv(near_col.at[past, pl.ds(1, col_close)], early_col.at[0])
    if col_close < cols - 1:
        wait_recv(far_col.at[past], early_col.at[1])
    wait_recv(by_owner.at[past, pl.ds(0, depth)], early_share)

    def tile_rows(offset):
        source = at_col(rows_y - offset[0], rows_x - offset[1])
        return pl.ds(pl.multiple_of(source * width, width), width)

    def backward(s, t, blocks, offsets):
        when = t + DEL - 1 - pair_ref[s, 3]
        mine = pair_ref[s, 0]
        total = None
        for first in range(0, len(offsets), 2):
            span = range(first, min(first + 2, len(offsets)))
            near = [blocks[when, k, mine] for k in span]
            tile = [tiles[tile_rows(offsets[k]), s * width : (s + 1) * width] for k in span]
            part = jnp.dot(
                jnp.concatenate(near, axis=1),
                jnp.concatenate(tile, axis=0),
                preferred_element_type=jnp.float32,
            )
            total = part if total is None else total + part
        return total

    def combine(side, dz, l):
        base = ((side * depth + dz) * clusters + l) * SM
        total = product[table[base]]
        for k in range(1, SM):
            total += product[table[base + k]]
        return total

    def step(t, carry):
        times = pl.ds(DEL - 1 + t, 1)

        def owner_sem(k):
            return owner_recv.at[t, k]

        for dz in z_near:
            if z_distance(dz) <= 3:
                share(times, dz, owner_sem, share_recv.at[t])
        wait_recv(near_col.at[times, pl.ds(1, col_close)], col_recv.at[t, 0])
        near_offsets = [(0, 0)] + col_near[:col_close]
        for s in range(slots):
            product[s] = backward(s, t, near_col, near_offsets)
        for dz in z_near:
            if z_distance(dz) > 3:
                share(times, dz, owner_sem, share_recv.at[t])
        far_offsets = col_near[col_close:]
        if far_offsets:
            wait_recv(far_col.at[times], col_recv.at[t, 1])
            for s in range(slots):
                product[s] += backward(s, t, far_col, far_offsets)
        for dz in range(depth):
            for l in range(clusters):
                sibling_out[t, dz, l] = combine(1, dz, l).astype(WIRE)

        wait_recv(by_owner.at[times, pl.ds(0, depth)], share_recv.at[t])
        for s in range(slots):
            when = t + DEL - 1 - pair_ref[s, 3]
            block = by_owner[when, pair_ref[s, 1], pair_ref[s, 2]]
            for l in range(clusters):
                chosen = (pair_ref[s, 4] == 1) & (pair_ref[s, 0] == l)
                lhs[l * 32 : (l + 1) * 32, s * width : (s + 1) * width] = jnp.where(
                    chosen, block, jnp.zeros_like(block)
                )
        copy(
            sibling_out.at[t], sibling_in.at[t], sum_send, sibling_recv.at[t], sibling
        ).start()

        left = lhs[...]

        def forward(offset):
            return jnp.dot(
                left, turned[at_col(*offset)], preferred_element_type=jnp.float32
            ).reshape(clusters, 32, width)

        def send_forward(offset, part):
            index = col_near.index(offset)
            forward_out[t, index] = part.astype(WIRE)
            copy(
                forward_out.at[t, index],
                forward_in.at[t, index],
                sum_send,
                forward_recv.at[t, 0 if index < col_close else 1],
                (pair, at_col(*offset)),
            ).start()

        waiting = []
        for offset in col_far:
            waiting.append((offset, forward(offset)))
            if len(waiting) > AHEAD:
                send_forward(*waiting.pop(0))
        field = forward((0, 0))
        for item in waiting:
            send_forward(*item)
        for dz in range(depth):
            for l in range(clusters):
                own_back[dz, l] = combine(0, dz, l)

        wait_recv(sibling_in.at[t], sibling_recv.at[t])
        for dz in z_far:
            total = own_back[dz] + sibling_in[t, dz].astype(jnp.float32)
            index = z_near.index(dz)
            back_out[t, index] = total.astype(WIRE)
            copy(
                back_out.at[t, index],
                back_in.at[t, index],
                sum_send,
                back_recv.at[t, 0 if index < z_close else 1],
                (at_z(dz), col),
            ).start()
        field = field + own_back[0] + sibling_in[t, 0].astype(jnp.float32)

        def collect(field, ref, first, last, sem):
            if last > first:
                wait_recv(ref.at[t, pl.ds(first, last - first)], sem)
                for index in range(first, last):
                    field = field + ref[t, index].astype(jnp.float32)
            return field

        field = collect(field, forward_in, 0, col_close, forward_recv.at[t, 0])
        field = collect(field, back_in, 0, z_close, back_recv.at[t, 0])
        field = collect(field, forward_in, col_close, cols - 1, forward_recv.at[t, 1])
        field = collect(field, back_in, z_close, depth - 1, back_recv.at[t, 1])
        fresh = (excitation[t] - field) / diagonal[...][:, None, :]
        out_ref[t] = fresh

        @pl.when(t < STEPS - 1)
        def publish():
            rounded = fresh.astype(jnp.bfloat16)
            by_owner[DEL + t, pair] = rounded
            near_col[DEL + t, 0] = rounded
            send_step(t + 1)

        return carry

    lax.fori_loop(0, STEPS, step, 0)

    def sent(count, sem):
        copy(drain.at[pl.ds(0, count)], drain.at[pl.ds(0, count)], sem, early_share, sibling).wait_send()

    times = DEL + STEPS - 1
    sent(times * (2 * depth - 1), density_send)
    sent(times * (cols - 1), col_send)
    sent(STEPS * (cols - 1 + depth + depth - 1), sum_send)


def march(groups, cols, pair_list, near_tile_block, history, excitation, diagonal):
    slots, patches, width = near_tile_block.shape
    clusters, excite = history.shape[1:3]
    depth = groups // 2
    rows_y = rows_x = math.isqrt(cols)
    block = (clusters, excite, width)
    near = 1 + sum(
        0 < ring_distance(dy, rows_y) + ring_distance(dx, rows_x) <= 2
        for dy in range(rows_y)
        for dx in range(rows_x)
    )
    dma = pltpu.SemaphoreType.DMA
    anywhere = pl.BlockSpec(memory_space=pl.ANY)
    return pl.pallas_call(
        functools.partial(kernel, (depth, rows_y, rows_x, slots, clusters)),
        out_shape=jax.ShapeDtypeStruct((STEPS,) + block, jnp.float32),
        in_specs=[pl.BlockSpec(memory_space=pltpu.SMEM)] + [anywhere] * 4,
        out_specs=pl.BlockSpec(memory_space=pltpu.VMEM),
        scratch_shapes=[
            pltpu.VMEM((patches, slots * width), jnp.bfloat16),
            pltpu.VMEM((cols, slots * width, width), jnp.bfloat16),
            pltpu.VMEM((DEL,) + block, jnp.float32),
            pltpu.VMEM((STEPS,) + block, jnp.float32),
            pltpu.VMEM((clusters, width), jnp.float32),
            pltpu.VMEM((DEL + STEPS - 1, groups) + block, jnp.bfloat16),
            pltpu.VMEM((DEL + STEPS - 1, near) + block, jnp.bfloat16),
            pltpu.VMEM((DEL + STEPS - 1, max(cols - near, 1)) + block, jnp.bfloat16),
            pltpu.VMEM((STEPS * (cols + 2 * depth),) + block, WIRE),
            pltpu.VMEM((clusters * excite, slots * width), jnp.bfloat16),
            pltpu.SMEM((groups * clusters * SM,), jnp.int32),
            pltpu.VMEM((slots + 1, excite, width), jnp.float32),
            pltpu.VMEM((depth,) + block, jnp.float32),
            pltpu.VMEM((STEPS, cols - 1) + block, WIRE),
            pltpu.VMEM((STEPS, cols - 1) + block, WIRE),
            pltpu.VMEM((STEPS, depth) + block, WIRE),
            pltpu.VMEM((STEPS, depth) + block, WIRE),
            pltpu.VMEM((STEPS, depth - 1) + block, WIRE),
            pltpu.VMEM((STEPS, depth - 1) + block, WIRE),
            dma((4,)),
            dma,
            dma,
            dma,
            dma((depth - 1,)),
            dma,
            dma((2,)),
            dma((STEPS, depth - 1)),
            dma((STEPS,)),
            dma((STEPS, 2)),
            dma((STEPS, 2)),
            dma((STEPS,)),
            dma((STEPS, 2)),
        ],
        compiler_params=pltpu.CompilerParams(collective_id=0, has_side_effects=True),
    )(pair_list, near_tile_block, history, excitation, diagonal)


def solution(mesh):
    placed = (
        P("pairs", None),
        P("pairs", None, "cols"),
        P(None, "pairs", None, "cols"),
        P(None, "pairs", None, "cols"),
        P("pairs", "cols"),
    )
    return jax.shard_map(
        functools.partial(march, mesh.shape["pairs"], mesh.shape["cols"]),
        mesh=mesh,
        in_specs=placed,
        out_specs=P(None, "pairs", None, "cols"),
        check_vma=False,
    )
```

time: 84.2 us -> 76.7 us (0.911)
  Pallas kernels: 83.3 us -> 75 us
    pallas_call x1, Pallas kernels: 83.3 us -> 75 us  [march(): pl.pallas_call(functools.partial(kernel, (depth, rows_y, rows_x, slots, c...]
where the time goes in v2:
time: 76.7 us; the launch traced here: 76.6 us
  Pallas kernels  75 us (98%)
  local copies, waits for them, and re-layouts  1.57 us (2%)
    pallas_call x1, Pallas kernels, march(): pl.pallas_call(functools.partial(kernel, (depth, rows_y, rows_x, slots, c...  75 us
    unnamed x1, local copies, waits for them, and re-layouts  1.57 us

profile of v2, /device:TPU:1, one launch (start us, length us, event | category | flops | bytes accessed | tf_op | source)
XLA Modules:
  0.0 76.6 jit_solution(10399193309366064269)
XLA Ops:
  0.0 75.0 %shard_map.55 = f32[4,2,32,128]{3,2,1,0:T(8,128)} custom-call(s32[6,5]{1,0:T(8,128)} %pair_ref.1, bf16[6,2048,128]{2,1,0:T(8,128)(2,1)} %tile_hbm.1, f32[4,2,32,128]{3,2,1,0:T(8,128)} %history_hbm.1, f32[4,2,32,128]{3,2,1,0:T(8,128)} %excitation_hbm.1, f32[2,128]{1,0:T(2,128)} %diagonal_hbm.1), custom_call_target="tpu_custom_call" | custom-call | tf_op jit(solution)/shard_map/pallas_call | solution.py:366
  75.0 1.6 %copy.7 = f32[4,2,32,128]{3,2,1,0:T(8,128)} copy(f32[4,2,32,128]{3,2,1,0:T(8,128)} %shard_map.55) | data formatting | bytes 262144

commit v3 on v2

v3 whole, which is shorter than its diff:
```python
import functools
import math

import jax
import jax.numpy as jnp
from jax import lax
from jax.experimental import pallas as pl
from jax.experimental.pallas import tpu as pltpu
from jax.sharding import PartitionSpec as P

MESH = pl.DeviceIdType.MESH
STEPS = 4
DEL = 4
SM = 3
AHEAD = 2
WIRE = jnp.bfloat16


def ring_distance(offset, size):
    return min(offset, size - offset)


def kernel(
    sizes,
    pair_hbm,
    tile_hbm,
    history_hbm,
    excitation_hbm,
    diagonal_hbm,
    out_ref,
    pairs,
    tiles,
    turned,
    history,
    excitation,
    diagonal,
    by_z,
    near_col,
    far_col,
    drain,
    lhs,
    table,
    product,
    fresh_out,
    fresh_in,
    forward_out,
    forward_in,
    back_out,
    back_in,
    local_sem,
    swap_recv,
    swap_send,
    density_send,
    sum_send,
    fresh_send,
    fresh_recv,
    early_z,
    early_col,
    z_recv,
    col_recv,
    forward_recv,
    back_recv,
):
    depth, rows_y, rows_x, slots, clusters, half = sizes
    cols = rows_y * rows_x
    width = 128
    count = 2 * clusters
    stack = 2 * slots
    pair = lax.axis_index("pairs")
    col = lax.axis_index("cols")
    z, core = pair // 2, lax.rem(pair, 2)
    y, x = col // rows_x, lax.rem(col, rows_x)
    sibling = (z * 2 + 1 - core, col)

    def at_z(dz):
        return lax.rem(z + dz, depth)

    def z_device(dz):
        return (at_z(dz) * 2 + core, col)

    def at_col(dy, dx):
        return lax.rem(y + dy, rows_y) * rows_x + lax.rem(x + dx, rows_x)

    def z_distance(dz):
        return ring_distance(dz, depth)

    def col_distance(d):
        return ring_distance(d[0], rows_y) + ring_distance(d[1], rows_x)

    z_near = sorted(range(1, depth), key=z_distance)
    z_far = z_near[::-1]
    col_near = sorted(
        [(dy, dx) for dy in range(rows_y) for dx in range(rows_x)][1:], key=col_distance
    )
    col_far = col_near[::-1]
    z_close = sum(z_distance(d) <= 2 for d in z_near)
    col_close = sum(col_distance(d) <= 2 for d in col_near)
    peers = [z_device(dz) for dz in z_far] + [sibling]
    peers += [(pair, at_col(dy, dx)) for dy, dx in col_far]

    barrier = pltpu.get_barrier_semaphore()
    for peer in peers:
        pl.semaphore_signal(barrier, inc=1, device_id=peer, device_id_type=MESH)

    mine = pl.ds(core * clusters, clusters)
    kept = pl.ds(pl.multiple_of(core * half, half), half)
    given = pl.ds(pl.multiple_of((1 - core) * half, half), half)

    def column(s):
        return pl.ds(pl.multiple_of((core * slots + s) * width, width), width)

    loads = [
        pltpu.make_async_copy(
            history_hbm.at[:, :, kept, :], history.at[:, mine], local_sem.at[0]
        ),
        pltpu.make_async_copy(pair_hbm, pairs.at[core], local_sem.at[1]),
        pltpu.make_async_copy(
            excitation_hbm.at[:, :, kept, :], excitation.at[:, mine], local_sem.at[2]
        ),
        pltpu.make_async_copy(diagonal_hbm, diagonal.at[core], local_sem.at[3]),
    ]
    for load in loads:
        load.start()
    for s in range(slots):
        pltpu.make_async_copy(
            tile_hbm.at[s], tiles.at[:, column(s)], local_sem.at[4]
        ).start()

    def round_history(who):
        part = pl.ds(who * clusters, clusters)
        for d in range(DEL):
            rounded = history[d, part].astype(jnp.bfloat16)
            by_z[DEL - 1 - d, z, part] = rounded
            near_col[DEL - 1 - d, 0, part] = rounded

    loads[0].wait()
    round_history(core)

    pl.semaphore_wait(barrier, len(peers))

    def copy(src, dst, send, recv, device):
        return pltpu.make_async_remote_copy(
            src_ref=src,
            dst_ref=dst,
            send_sem=send,
            recv_sem=recv,
            device_id=device,
            device_id_type=MESH,
        )

    swaps = [
        copy(
            history_hbm.at[:, :, given, :],
            history.at[:, mine],
            swap_send.at[0],
            swap_recv.at[0],
            sibling,
        ),
        copy(pair_hbm, pairs.at[core], swap_send.at[1], swap_recv.at[1], sibling),
        copy(
            excitation_hbm.at[:, :, given, :],
            excitation.at[:, mine],
            swap_send.at[2],
            swap_recv.at[2],
            sibling,
        ),
        copy(diagonal_hbm, diagonal.at[core], swap_send.at[3], swap_recv.at[3], sibling),
    ]
    for swap in swaps:
        swap.start()

    def arrival(times, index, part):
        if index < col_close:
            return near_col.at[times, index + 1, part]
        return far_col.at[times, index - col_close, part]

    def send_density(times, part, z_sem, col_sem):
        source = by_z.at[times, z, part]
        for dz in z_far:
            copy(source, source, density_send, z_sem, z_device(dz)).start()
        for offset in col_far:
            index = col_near.index(offset)
            group = 0 if index < col_close else 1
            target = (pair, at_col(*offset))
            sem = col_sem(group)
            copy(source, arrival(times, index, part), density_send, sem, target).start()

    def wait_recv(ref, sem):
        copy(ref, ref, density_send, sem, sibling).wait_recv()

    def early_col_sem(group):
        return early_col.at[group]

    past = pl.ds(0, DEL)
    send_density(past, mine, early_z, early_col_sem)
    for s in range(slots):
        copy(
            tile_hbm.at[s], tiles.at[:, column(s)], swap_send.at[4], swap_recv.at[4], sibling
        ).start()
    swaps[0].wait_recv()
    round_history(1 - core)
    send_density(past, pl.ds((1 - core) * clusters, clusters), early_z, early_col_sem)

    for load in loads[1:]:
        load.wait()
    for swap in swaps[1:]:
        swap.wait_recv()

    def field_of(s, k):
        return pairs[s // slots, s % slots, k]

    keys = [
        jnp.where(field_of(s, 4) == 1, field_of(s, 1) * clusters + field_of(s, 2), -1)
        for s in range(stack)
    ]

    def place(n, carry):
        dz, rest = n // count, lax.rem(n, count)
        key = at_z(dz) * count + rest
        seen = jnp.int32(0)
        found = [jnp.int32(stack)] * (2 * SM)
        for s in range(stack):
            hit = keys[s] == key
            found = [jnp.where(hit & (seen == k), s, found[k]) for k in range(2 * SM)]
            seen = jnp.where(hit, seen + 1, seen)
        for k in range(2 * SM):
            table[n * 2 * SM + k] = found[k]
        return carry

    lax.fori_loop(0, depth * count, place, 0)
    product[stack] = jnp.zeros_like(product[stack])

    def turn(who):
        part = pl.ds(pl.multiple_of(who * slots * width, width), slots * width)

        def body(c, carry):
            rows = pl.ds(pl.multiple_of(c * width, width), width)
            turned[c, part, :] = tiles[rows, part].T
            return carry

        lax.fori_loop(0, cols, body, 0)

    held = tiles.at[:, pl.ds(0, slots * width)]
    pltpu.make_async_copy(held, held, local_sem.at[4]).wait()
    turn(core)
    wait_recv(held, swap_recv.at[4])
    turn(1 - core)

    wait_recv(near_col.at[past, pl.ds(1, col_close)], early_col.at[0])
    if col_close < cols - 1:
        wait_recv(far_col.at[past], early_col.at[1])
    wait_recv(by_z.at[past, pl.ds(0, depth - 1)], early_z)

    def tile_rows(offset):
        source = at_col(rows_y - offset[0], rows_x - offset[1])
        return pl.ds(pl.multiple_of(source * width, width), width)

    def backward(s, t, blocks, offsets):
        when = t + DEL - 1 - field_of(s, 3)
        which = s // slots * clusters + field_of(s, 0)
        total = None
        for first in range(0, len(offsets), 2):
            span = range(first, min(first + 2, len(offsets)))
            near = [blocks[when, k, which] for k in span]
            tile = [tiles[tile_rows(offsets[k]), s * width : (s + 1) * width] for k in span]
            part = jnp.dot(
                jnp.concatenate(near, axis=1),
                jnp.concatenate(tile, axis=0),
                preferred_element_type=jnp.float32,
            )
            total = part if total is None else total + part
        return total

    def combine(dz, j):
        base = (dz * count + j) * 2 * SM
        total = product[table[base]]
        for k in range(1, 2 * SM):
            total += product[table[base + k]]
        return total

    def step(t, carry):
        times = pl.ds(DEL - 1 + t, 1)

        @pl.when(t > 0)
        def near_arrived():
            wait_recv(near_col.at[times, pl.ds(1, col_close)], col_recv.at[t, 0])

        near_offsets = [(0, 0)] + col_near[:col_close]
        for s in range(stack):
            product[s] = backward(s, t, near_col, near_offsets)

        @pl.when(t > 0)
        def z_arrived():
            wait_recv(by_z.at[times, pl.ds(0, depth - 1)], z_recv.at[t])

        for s in range(stack):
            when = t + DEL - 1 - field_of(s, 3)
            owner = field_of(s, 1)
            which = lax.rem(owner, 2) * clusters + field_of(s, 2)
            block = by_z[when, owner // 2, which]
            for l in range(clusters):
                chosen = (field_of(s, 4) == 1) & (field_of(s, 0) == l)
                for who in range(2):
                    row = (who * clusters + l) * half
                    value = jnp.zeros_like(block)
                    if who == s // slots:
                        value = jnp.where(chosen, block, value)
                    lhs[row : row + half, s * width : (s + 1) * width] = value

        far_offsets = col_near[col_close:]
        if far_offsets:

            @pl.when(t > 0)
            def far_arrived():
                wait_recv(far_col.at[times], col_recv.at[t, 1])

            for s in range(stack):
                product[s] += backward(s, t, far_col, far_offsets)

        for dz in z_far:
            index = z_near.index(dz)
            for j in range(count):
                back_out[t, index, j] = combine(dz, j).astype(WIRE)
            copy(
                back_out.at[t, index],
                back_in.at[t, index],
                sum_send,
                back_recv.at[t, 0 if index < z_close else 1],
                z_device(dz),
            ).start()

        left = lhs[...]

        def forward(offset):
            return jnp.dot(
                left, turned[at_col(*offset)], preferred_element_type=jnp.float32
            ).reshape(count, half, width)

        def send_forward(offset, part):
            index = col_near.index(offset)
            forward_out[t, index] = part.astype(WIRE)
            copy(
                forward_out.at[t, index],
                forward_in.at[t, index],
                sum_send,
                forward_recv.at[t, 0 if index < col_close else 1],
                (pair, at_col(*offset)),
            ).start()

        waiting = []
        for offset in col_far:
            waiting.append((offset, forward(offset)))
            if len(waiting) > AHEAD:
                send_forward(*waiting.pop(0))
        field = forward((0, 0))
        for item in waiting:
            send_forward(*item)
        field = field + jnp.stack([combine(0, j) for j in range(count)])

        def collect(field, ref, first, last, sem):
            if last > first:
                wait_recv(ref.at[t, pl.ds(first, last - first)], sem)
                for index in range(first, last):
                    field = field + ref[t, index].astype(jnp.float32)
            return field

        field = collect(field, back_in, 0, z_close, back_recv.at[t, 0])
        field = collect(field, back_in, z_close, depth - 1, back_recv.at[t, 1])
        field = collect(field, forward_in, 0, col_close, forward_recv.at[t, 0])
        field = collect(field, forward_in, col_close, cols - 1, forward_recv.at[t, 1])
        weights = diagonal[...].reshape(count, 1, width)
        fresh = (excitation[t] - field) / weights
        fresh_out[t] = fresh

        @pl.when(t < STEPS - 1)
        def publish():
            rounded = fresh.astype(jnp.bfloat16)
            by_z[DEL + t, z] = rounded
            near_col[DEL + t, 0] = rounded
            send_density(
                pl.ds(DEL + t, 1),
                pl.ds(0, count),
                z_recv.at[t + 1],
                lambda group: col_recv.at[t + 1, group],
            )

        copy(
            fresh_out.at[t, pl.ds((1 - core) * clusters, clusters)],
            fresh_in.at[t],
            fresh_send,
            fresh_recv,
            sibling,
        ).start()
        out_ref[t, :, kept, :] = fresh_out[t, mine]
        return carry

    lax.fori_loop(0, STEPS, step, 0)

    def sent(ref, sem):
        copy(ref, ref, sem, fresh_recv, sibling).wait_send()

    for swap in swaps:
        swap.wait_send()
    sent(held, swap_send.at[4])
    sent(drain.at[pl.ds(0, (DEL + STEPS - 1) * (depth - 1 + cols - 1))], density_send)
    sent(drain.at[pl.ds(0, STEPS * (depth - 1 + cols - 1))], sum_send)
    sent(fresh_in, fresh_send)
    wait_recv(fresh_in, fresh_recv)
    for t in range(STEPS):
        out_ref[t, :, given, :] = fresh_in[t]


def march(groups, cols, pair_list, near_tile_block, history, excitation, diagonal):
    slots, patches, width = near_tile_block.shape
    clusters, excite = history.shape[1:3]
    depth = groups // 2
    half = excite // 2
    rows_y = rows_x = math.isqrt(cols)
    near = 1 + sum(
        0 < ring_distance(dy, rows_y) + ring_distance(dx, rows_x) <= 2
        for dy in range(rows_y)
        for dx in range(rows_x)
    )
    block = (2 * clusters, half, width)
    dma = pltpu.SemaphoreType.DMA
    times = DEL + STEPS - 1
    anywhere = pl.BlockSpec(memory_space=pl.ANY)
    return pl.pallas_call(
        functools.partial(kernel, (depth, rows_y, rows_x, slots, clusters, half)),
        out_shape=OUT((STEPS, clusters, excite, width), jnp.float32),
        in_specs=[anywhere] * 5,
        out_specs=pl.BlockSpec(memory_space=pltpu.VMEM),
        scratch_shapes=[
            pltpu.SMEM((2,) + pair_list.shape, jnp.int32),
            pltpu.VMEM((patches, 2 * slots * width), jnp.bfloat16),
            pltpu.VMEM((cols, 2 * slots * width, width), jnp.bfloat16),
            pltpu.VMEM((DEL,) + block, jnp.float32),
            pltpu.VMEM((STEPS,) + block, jnp.float32),
            pltpu.VMEM((2, clusters, width), jnp.float32),
            pltpu.VMEM((times, depth) + block, jnp.bfloat16),
            pltpu.VMEM((times, near) + block, jnp.bfloat16),
            pltpu.VMEM((times, max(cols - near, 1)) + block, jnp.bfloat16),
            pltpu.VMEM((times * (depth + cols),) + block, WIRE),
            pltpu.VMEM((2 * clusters * half, 2 * slots * width), jnp.bfloat16),
            pltpu.SMEM((depth * 2 * clusters * 2 * SM,), jnp.int32),
            pltpu.VMEM((2 * slots + 1, half, width), jnp.float32),
            pltpu.VMEM((STEPS,) + block, jnp.float32),
            pltpu.VMEM((STEPS, clusters, half, width), jnp.float32),
            pltpu.VMEM((STEPS, cols - 1) + block, WIRE),
            pltpu.VMEM((STEPS, cols - 1) + block, WIRE),
            pltpu.VMEM((STEPS, depth - 1) + block, WIRE),
            pltpu.VMEM((STEPS, depth - 1) + block, WIRE),
            dma((5,)),
            dma((5,)),
            dma((5,)),
            dma,
            dma,
            dma,
            dma,
            dma,
            dma((2,)),
            dma((STEPS,)),
            dma((STEPS, 2)),
            dma((STEPS, 2)),
            dma((STEPS, 2)),
        ],
        compiler_params=pltpu.CompilerParams(collective_id=0, has_side_effects=True),
    )(pair_list, near_tile_block, history, excitation, diagonal)


OUT = pltpu.VMEM


def solution(mesh):
    placed = (
        P("pairs", None),
        P("pairs", None, "cols"),
        P(None, "pairs", None, "cols"),
        P(None, "pairs", None, "cols"),
        P("pairs", "cols"),
    )
    return jax.shard_map(
        functools.partial(march, mesh.shape["pairs"], mesh.shape["cols"]),
        mesh=mesh,
        in_specs=placed,
        out_specs=P(None, "pairs", None, "cols"),
        check_vma=False,
    )
```

time: 76.7 us -> 71.3 us (0.930)
  Pallas kernels: 75 us -> 70.6 us
  local copies, waits for them, and re-layouts: 1.57 us -> 0.66 us
    pallas_call x1, Pallas kernels: 75 us -> 70.6 us  [march(): pl.pallas_call(functools.partial(kernel, (depth, rows_y, rows_x, slots, c...]
    unnamed x1, local copies, waits for them, and re-layouts: 1.57 us -> 0.66 us
where the time goes in v3:
time: 71.3 us
  Pallas kernels  70.6 us (99%)
    pallas_call x1, Pallas kernels, march(): pl.pallas_call(functools.partial(kernel, (depth, rows_y, rows_x, slots, c...  70.6 us

profile of v3, /device:TPU:1, one launch (start us, length us, event | category | flops | bytes accessed | tf_op | source)
XLA Modules:
  0.0 71.3 jit_solution(9048538838793274596)
XLA Ops:
  0.0 70.6 %shard_map.55 = f32[4,2,32,128]{3,2,1,0:T(8,128)S(1)} custom-call(s32[6,5]{1,0:T(8,128)} %pair_hbm.1, bf16[6,2048,128]{2,1,0:T(8,128)(2,1)} %tile_hbm.1, f32[4,2,32,128]{3,2,1,0:T(8,128)} %history_hbm.1, f32[4,2,32,128]{3,2,1,0:T(8,128)} %excitation_hbm.1, f32[2,128]{1,0:T(2,128)} %diagonal_hbm.1), custom_call_target="tpu_custom_call" | custom-call | tf_op jit(solution)/shard_map/pallas_call | solution.py:428
  70.6 0.7 copy.7

commit v4 on v3

--- a/solution.py
+++ b/solution.py
@@ -56,6 +56,8 @@
     fresh_recv,
     early_z,
     early_col,
+    early_relay,
+    early_turn,
     z_recv,
     col_recv,
     forward_recv,
@@ -188,18 +190,54 @@
     def wait_recv(ref, sem):
         copy(ref, ref, density_send, sem, sibling).wait_recv()
 
-    def early_col_sem(group):
-        return early_col.at[group]
-
     past = pl.ds(0, DEL)
-    send_density(past, mine, early_z, early_col_sem)
+    relay_z = [dz for dz in z_near if z_distance(dz) == 2] if depth == 8 else []
+    direct_z = [dz for dz in z_far if z_distance(dz) <= 2 or not relay_z]
+    x_line = [(0, dx) for dx in range(1, rows_x)]
+    y_line = [(dy, 0) for dy in range(1, rows_y)]
+    lines = [offset for offset in col_far if 0 in offset]
+
+    def early_first(way, part):
+        source = by_z.at[past, z, part]
+        for dz in direct_z:
+            sem = early_z
+            if dz in relay_z:
+                sem = early_relay.at[way, relay_z.index(dz)]
+            copy(source, source, density_send, sem, z_device(dz)).start()
+        first = x_line if way == 0 else y_line
+        for offset in lines:
+            sem = early_col
+            if offset in first:
+                sem = early_turn.at[way, first.index(offset)]
+            target = arrival(past, col_near.index(offset), part)
+            copy(source, target, density_send, sem, (pair, at_col(*offset))).start()
+
+    def early_relays(way, part):
+        first, second = (x_line, y_line) if way == 0 else (y_line, x_line)
+        for start in sorted(first, key=col_distance):
+            block = arrival(past, col_near.index(start), part)
+            wait_recv(block, early_turn.at[way, first.index(start)])
+            for then in sorted(second, key=lambda d: -col_distance(d)):
+                final = (start[0] + then[0], start[1] + then[1])
+                target = arrival(past, col_near.index(final), part)
+                copy(block, target, density_send, early_col, (pair, at_col(*then))).start()
+        for index, dz in enumerate(relay_z):
+            block = by_z.at[past, at_z(depth - dz), part]
+            wait_recv(block, early_relay.at[way, index])
+            unit = dz // 2 if dz == 2 else depth - 1
+            if (dz == 2) == (way == 0):
+                copy(block, block, density_send, early_z, z_device(dz)).start()
+            copy(block, block, density_send, early_z, z_device(unit)).start()
+
+    theirs = pl.ds((1 - core) * clusters, clusters)
+    early_first(0, mine)
     for s in range(slots):
         copy(
             tile_hbm.at[s], tiles.at[:, column(s)], swap_send.at[4], swap_recv.at[4], sibling
         ).start()
     swaps[0].wait_recv()
     round_history(1 - core)
-    send_density(past, pl.ds((1 - core) * clusters, clusters), early_z, early_col_sem)
+    early_first(1, theirs)
 
     for load in loads[1:]:
         load.wait()
@@ -242,14 +280,15 @@
 
     held = tiles.at[:, pl.ds(0, slots * width)]
     pltpu.make_async_copy(held, held, local_sem.at[4]).wait()
+    early_relays(0, mine)
+    early_relays(1, theirs)
     turn(core)
     wait_recv(held, swap_recv.at[4])
     turn(1 - core)
 
-    wait_recv(near_col.at[past, pl.ds(1, col_close)], early_col.at[0])
-    if col_close < cols - 1:
-        wait_recv(far_col.at[past], early_col.at[1])
-    wait_recv(by_z.at[past, pl.ds(0, depth - 1)], early_z)
+    others = DEL * (2 * (cols - 1) - len(x_line) - len(y_line)) // 2
+    wait_recv(drain.at[pl.ds(0, others)], early_col)
+    wait_recv(drain.at[pl.ds(0, DEL * (depth - 1 - len(relay_z)))], early_z)
 
     def tile_rows(offset):
         source = at_col(rows_y - offset[0], rows_x - offset[1])
@@ -458,7 +497,9 @@
             dma,
             dma,
             dma,
-            dma((2,)),
+            dma,
+            dma((2, 2)),
+            dma((2, rows_x - 1)),
             dma((STEPS,)),
             dma((STEPS, 2)),
             dma((STEPS, 2)),

time: 71.3 us -> 69.4 us (0.973)
  Pallas kernels: 70.6 us -> 68.7 us
    pallas_call x1, Pallas kernels: 70.6 us -> 68.7 us  [march(): pl.pallas_call(functools.partial(kernel, (depth, rows_y, rows_x, slots, c...]
where the time goes in v4:
time: 69.4 us
  Pallas kernels  68.7 us (99%)
    pallas_call x1, Pallas kernels, march(): pl.pallas_call(functools.partial(kernel, (depth, rows_y, rows_x, slots, c...  68.7 us

profile of v4, /device:TPU:1, one launch (start us, length us, event | category | flops | bytes accessed | tf_op | source)
XLA Modules:
  0.0 69.4 jit_solution(7978117517081536004)
XLA Ops:
  0.0 68.7 %shard_map.55 = f32[4,2,32,128]{3,2,1,0:T(8,128)S(1)} custom-call(s32[6,5]{1,0:T(8,128)} %pair_hbm.1, bf16[6,2048,128]{2,1,0:T(8,128)(2,1)} %tile_hbm.1, f32[4,2,32,128]{3,2,1,0:T(8,128)} %history_hbm.1, f32[4,2,32,128]{3,2,1,0:T(8,128)} %excitation_hbm.1, f32[2,128]{1,0:T(2,128)} %diagonal_hbm.1), custom_call_target="tpu_custom_call" | custom-call | tf_op jit(solution)/shard_map/pallas_call | solution.py:467
  68.7 0.7 copy.7

commit v5 on v4

--- a/solution.py
+++ b/solution.py
@@ -178,9 +178,15 @@
 
     def send_density(times, part, z_sem, col_sem):
         source = by_z.at[times, z, part]
+        for offset in col_far[:5]:
+            index = col_near.index(offset)
+            group = 0 if index < col_close else 1
+            target = (pair, at_col(*offset))
+            sem = col_sem(group)
+            copy(source, arrival(times, index, part), density_send, sem, target).start()
         for dz in z_far:
             copy(source, source, density_send, z_sem, z_device(dz)).start()
-        for offset in col_far:
+        for offset in col_far[5:]:
             index = col_near.index(offset)
             group = 0 if index < col_close else 1
             target = (pair, at_col(*offset))

time: 69.4 us -> 69 us (level)
  no operation moved by 1% of the time
where the time goes in v5:
time: 69 us; the launch traced here: 68.8 us
  Pallas kernels  68.1 us (99%)
    pallas_call x1, Pallas kernels, march(): pl.pallas_call(functools.partial(kernel, (depth, rows_y, rows_x, slots, c...  68.1 us

profile of v5, /device:TPU:1, one launch (start us, length us, event | category | flops | bytes accessed | tf_op | source)
XLA Modules:
  0.0 68.8 jit_solution(2598073563002596353)
XLA Ops:
  0.0 68.1 %shard_map.55 = f32[4,2,32,128]{3,2,1,0:T(8,128)S(1)} custom-call(s32[6,5]{1,0:T(8,128)} %pair_hbm.1, bf16[6,2048,128]{2,1,0:T(8,128)(2,1)} %tile_hbm.1, f32[4,2,32,128]{3,2,1,0:T(8,128)} %history_hbm.1, f32[4,2,32,128]{3,2,1,0:T(8,128)} %excitation_hbm.1, f32[2,128]{1,0:T(2,128)} %diagonal_hbm.1), custom_call_target="tpu_custom_call" | custom-call | tf_op jit(solution)/shard_map/pallas_call | solution.py:473
  68.1 0.7 copy.7
